TPU v7x, 32 devices: a whole 2x2x4 slice. The times are simulated.
32 devices in a mesh: dir: 8 (over y, x, core), freq: 4 (over z).
Axes of the slice: x: 2, y: 2, z: 4, core: 2. Of those that a mesh axis runs over, the one named last changes fastest.
Arguments:
- observed: float32 [512, 8, 2, 2, 512], P('dir', 'freq'), as said below
- flags: int32 [512, 2, 512], P('dir'), may hold values from 0 to 1, as said below
- screen: float32 [16, 512], P('dir'), may hold values from -6 to 6
- screen_kernel: float32 [512, 512], replicated
- station_uv: float32 [2, 2, 512], replicated, may hold values from -360 to 360
- source_lm: float32 [2, 3072], P(None, 'dir'), may hold values from -0.05 to 0.05
- source_flux: float32 [3072], P('dir')
- station_gain: bfloat16 [8, 2, 2, 512, 3072], P('freq', None, None, None, 'dir'), may hold values from -4.1875 to 4.1875
- source_direction: int32 [3072], P('dir'), may hold values from 0 to 1
- freq_ratio: float32 [8], P('freq')
Outputs:
- residual: float32 [512, 8, 2, 2, 512], P('dir', 'freq')
- updated_screen: float32 [16, 512], P('dir')
Inputs may be any that keep to these rules, and one draw needn't show every extreme that they name: observed is Hermitian in its stations: observed[p, f, t, 0, q] equals observed[q, f, t, 0, p] and observed[p, f, t, 1, q] equals minus observed[q, f, t, 1, p]. flags[p, t, q] equals flags[q, t, p].
All inputs are finite; a program needn't handle non-finite values.
Results may differ from a plain program's by a relative error of at most 0.0037.
Values may be sent and summed in bfloat16 or wider, within the bound.
A program may use at most 128 MiB of HBM per device.

v0:
```python
import math
import jax
import jax.numpy as jnp
from jax import lax
from jax.sharding import PartitionSpec as P

step_size = 0.3
epsilon = 1e-06
highest = lax.Precision.HIGHEST


def body(
    observed,
    flags,
    screen,
    screen_kernel,
    station_uv,
    source_lm,
    source_flux,
    station_gain,
    source_direction,
    freq_ratio,
):
    dir_count = lax.axis_size("dir")
    stations = screen.shape[1]
    local_dirs = screen.shape[0]
    local_sources = source_flux.shape[0]
    local_rows = observed.shape[0]
    channels = freq_ratio.shape[0]
    times_count = station_uv.shape[0]
    matrices = channels * times_count
    scaling = 1.0 / math.sqrt(local_sources * dir_count)
    onehot_dirs = (
        source_direction[:, None] == jnp.arange(local_dirs, dtype=jnp.int32)[None, :]
    ).astype(jnp.float32)
    screen_src = jnp.einsum("dp,kd->pk", screen, onehot_dirs, precision=highest)
    freq_each = jnp.repeat(freq_ratio, times_count)
    uv_each = jnp.tile(station_uv, (channels, 1, 1))
    geometry = jnp.einsum("mcp,ck->pmk", uv_each, source_lm, precision=highest)
    phase_angle = (
        screen_src[:, None, :] / freq_each[None, :, None]
        + (2.0 * math.pi * freq_each)[None, :, None] * geometry
    )
    gain_all = station_gain.reshape(matrices, 2, stations, local_sources).astype(jnp.float32)
    gain_re = jnp.transpose(gain_all[:, 0], (1, 0, 2))
    gain_im = jnp.transpose(gain_all[:, 1], (1, 0, 2))
    cosine = jnp.cos(phase_angle)
    sine = jnp.sin(phase_angle)
    amplitude = jnp.sqrt(source_flux)[None, None, :]
    phasor_re = (amplitude * (gain_re * cosine - gain_im * sine)).astype(jnp.bfloat16)
    phasor_im = (amplitude * (gain_re * sine + gain_im * cosine)).astype(jnp.bfloat16)
    left_mat = jnp.concatenate([phasor_re, phasor_im], axis=2)
    skew_mat = jnp.concatenate([phasor_im, -phasor_re], axis=2)
    real_part = jnp.einsum("pmk,qmk->pmq", left_mat, left_mat, preferred_element_type=jnp.float32)
    imag_part = jnp.einsum("pmk,qmk->pmq", skew_mat, left_mat, preferred_element_type=jnp.float32)
    packed_rows = lax.psum_scatter(
        (real_part + imag_part) * scaling, "dir", scatter_dimension=0, tiled=True
    )
    mirrored = lax.all_to_all(packed_rows, "dir", split_axis=2, concat_axis=0, tiled=True)
    mirrored = jnp.transpose(mirrored, (2, 1, 0))
    model_rows = jnp.stack([(packed_rows + mirrored) * 0.5, (packed_rows - mirrored) * 0.5], axis=2)
    row_ids = lax.axis_index("dir") * local_rows + jnp.arange(local_rows, dtype=jnp.int32)
    cross_baseline = (row_ids[:, None] != jnp.arange(stations, dtype=jnp.int32)[None, :]).astype(
        jnp.float32
    )
    baseline_keep = (
        jnp.tile(flags, (1, channels, 1)).astype(jnp.float32) * cross_baseline[:, None, :]
    )
    obs_rows = observed.reshape(local_rows, matrices, 2, stations)
    residual = baseline_keep[:, :, None, :] * (obs_rows - model_rows)
    resid_half = residual.astype(jnp.bfloat16)
    forward_mat = jnp.stack([left_mat, -skew_mat], axis=2)
    conj_mat = jnp.concatenate([phasor_re, -phasor_im], axis=2)
    dual_mat = jnp.concatenate([phasor_im, phasor_re], axis=2)
    adjoint_mat = jnp.stack([conj_mat, dual_mat], axis=2)
    rows_piece = lax.all_gather(resid_half, "dir", axis=0, tiled=True)
    row_part = jnp.einsum(
        "rmwq,qmwk->rmk", rows_piece, forward_mat, preferred_element_type=jnp.float32
    )
    col_total = jnp.einsum(
        "rmwp,rmwk->pmk", rows_piece, adjoint_mat, preferred_element_type=jnp.float32
    )
    weight_re = row_part[..., :local_sources] + col_total[..., :local_sources]
    weight_im = row_part[..., local_sources:] - col_total[..., local_sources:]
    source_grad = (
        phasor_im.astype(jnp.float32) * weight_re - phasor_re.astype(jnp.float32) * weight_im
    )
    source_grad = source_grad * (scaling / freq_each)[None, :, None]
    local_grad = jnp.einsum("pmk,kd->dp", source_grad, onehot_dirs, precision=highest)
    entry_count = local_dirs * dir_count * stations
    total_grad = lax.psum(local_grad, "freq")
    smooth = jnp.dot(total_grad, screen_kernel, precision=highest)
    total_sq = lax.psum(jnp.sum(smooth * smooth), "dir")
    updated = screen - step_size * smooth * lax.rsqrt(total_sq / entry_count + epsilon)
    return (residual.reshape(observed.shape), updated)


def solution(mesh):
    placed = (
        P("dir", "freq", None, None, None),
        P("dir", None, None),
        P("dir", None),
        P(),
        P(),
        P(None, "dir"),
        P("dir"),
        P("freq", None, None, None, "dir"),
        P("dir"),
        P("freq"),
    )
    return jax.shard_map(
        body,
        mesh=mesh,
        in_specs=placed,
        out_specs=(P("dir", "freq", None, None, None), P("dir", None)),
        check_vma=False,
    )
```

profile of v0, /device:TPU:0, one launch (start us, length us, event | category | flops | bytes accessed | tf_op | source)
XLA Modules:
  0.0 248.1 jit_solution(14236749292300200952)
XLA Ops:
  7.2 0.8 broadcast_in_dim.2
  8.1 0.7 sqrt.3
  8.8 5.5 %copy.27 = f32[2,2,2,512,384]{3,4,1,0,2:T(8,128)} copy(bf16[2,2,2,512,384]{4,3,2,1,0:T(8,128)(2,1)} %param.17) | data formatting | bytes 9437184 | tf_op jit(solution)/shard_map/convert_element_type | solution.py:44
  14.3 0.5 convolution_bitcast_fusion
  14.9 14.2 %fusion.46 = (f32[512,4,384]{0,2,1:T(8,128)S(1)}, f32[512,4,384]{0,2,1:T(8,128)S(1)}) fusion(f32[4,2,512]{2,1,0:T(2,128)S(1)} %bitcast.86, f32[2,384]{1,0:T(2,128)S(1)} %copy-done.12, f32[4]{0:T(128)S(1)} %get-tuple-element.16, f32[4]{0:T(128)S(1)} %div.26, f32[512,384]{0,1:T(8,128)S(1)} %convolution_bitcast_fusion), kind=kOutput, calls=%fused_computation.68 | convolution fusion | flops 21233664 | bytes 7097376 | tf_op jit(solution)/shard_map/mcp,ck->pmk/dot_general | solution.py:39
  29.1 3.2 %fusion.45 = (bf16[512,4,384]{0,2,1:T(8,128)(2,1)}, bf16[512,4,384]{0,2,1:T(8,128)(2,1)S(1)}, bf16[512,4,1,384]{0,3,1,2:T(8,128)(2,1)}, bf16[512,4,384]{0,2,1:T(8,128)(2,1)S(1)}) fusion(f32[512,4,384]{0,2,1:T(8,128)S(1)} %get-tuple-element.10, f32[4,2,512,384]{2,3,0,1:T(8,128)S(1)} %bitcast.78, f32[512,4,384]{0,2,1:T(8,128)S(1)} %get-tuple-element.11, ...), kind=kLoop, calls=%fused_computation.67 | loop fusion | flops 9437184 | bytes 18875904 | tf_op jit(solution)/shard_map/neg | solution.py:73
  32.3 0.3 neg.16
  32.6 2.1 fusion.30
  34.7 3.5 %multiply_bitcast_fusion = f32[512,4,512]{0,2,1:T(8,128)} fusion(f32[4,512,512]{2,1,0:T(8,128)S(1)} %fusion.30, bf16[512,4,384]{0,2,1:T(8,128)(2,1)S(1)} %get-tuple-element.5, bf16[512,4,384]{0,2,1:T(8,128)(2,1)S(1)} %neg.16, bf16[512,4,384]{0,2,1:T(8,128)(2,1)S(1)} %get-tuple-element.7), kind=kOutput, calls=%fused_computation.8 | convolution fusion | flops 1625292800 | bytes 13107200 | tf_op jit(solution)/shard_map/pmk,qmk->pmq/dot_general | solution.py:55
  38.1 5.5 %copy.32 = f32[512,4,512]{2,1,0:T(4,128)} copy(f32[512,4,512]{0,2,1:T(8,128)} %multiply_bitcast_fusion) | data formatting | bytes 8388608 | tf_op jit(solution)/shard_map/mul | solution.py:57
  43.6 0.9 copy-done.8
  44.6 0.1 convert_element_type.42
  44.6 0.1 tile.6
  44.8 1.3 convert_element_type.49
  46.0 0.6 dynamic-slice
  47.3 80.0 %all-reduce.3.cloned.1.call-done = f32[512,4,512]{2,1,0:T(4,128)} async-done(((f32[512,4,512]{2,1,0:T(4,128)}), f32[512,4,512]{2,1,0:T(4,128)}) %all-reduce.3.cloned.1.call-update) | async-done | bytes 4194320
  127.3 1.1 constant_dynamic-slice_fusion
  128.4 1.3 copy.33
  129.7 3.0 %reshape.106 = f32[8,1,16384]{2,1,0:T(1,128)} reshape(f32[512,4,64]{2,1,0:T(4,128)} %bitcast.83) | data formatting | bytes 1048576
  132.7 3.5 %all-to-all-start = ((f32[8,1,16384]{2,1,0:T(1,128)}), f32[8,1,16384]{2,1,0:T(1,128)S(1)}, u32[]{:S(2)}, u32[]{:S(2)}) async-start(f32[8,1,16384]{2,1,0:T(1,128)} %reshape.106), calls=%async_computation | async-start | bytes 1048576 | tf_op jit(solution)/shard_map/all_to_all | solution.py:59
  136.2 0.2 all-gather.2.cloned.1.call-start
  136.5 2.0 broadcast_multiply_fusion
  138.5 7.4 %all-to-all-done = f32[8,1,16384]{2,1,0:T(1,128)S(1)} async-done(((f32[8,1,16384]{2,1,0:T(1,128)}), f32[8,1,16384]{2,1,0:T(1,128)S(1)}, u32[]{:S(2)}, u32[]{:S(2)}) %all-to-all-start) | async-done | bytes 524320 | tf_op jit(solution)/shard_map/all_to_all | solution.py:59
  145.9 0.8 copy-done.7
  146.7 0.5 broadcast.60
  147.2 2.9 %reduce = f32[8,16384]{1,0:T(8,128)S(1)} reduce(f32[8,1,16384]{2,1,0:T(1,128)} %copy-done.7, f32[]{:T(128)} %broadcast.60), dimensions={1}, to_apply=%all_to_all.13.reduce_sub_computation | reduce | bytes 1048580 | tf_op jit(solution)/shard_map/all_to_all | solution.py:59
  150.1 1.7 reshape.107
  151.8 2.8 %copy.64 = f32[64,4,8,64]{0,2,1,3:T(8,128)} copy(f32[64,4,8,64]{0,1,3,2:T(4,128)} %bitcast.84) | data formatting | bytes 1048576 | tf_op jit(solution)/shard_map/all_to_all | solution.py:59
  154.6 2.4 all_to_all.16
  156.9 1.4 fusion.34
  158.4 0.8 copy-done.5
  159.2 1.8 fusion.33
  161.0 1.0 copy.38
  162.0 4.4 %maximum_negate_fusion = bf16[512,4,1,768]{0,3,1,2:T(8,128)(2,1)} fusion(bf16[512,4,1,384]{0,3,1,2:T(8,128)(2,1)} %get-tuple-element.6, bf16[512,4,1,384]{0,3,1,2:T(8,128)(2,1)} %bitcast.79), kind=kLoop, calls=%fused_computation.29 | loop fusion | flops 7864320 | bytes 6291456 | tf_op jit(solution)/shard_map/neg | solution.py:72
  166.3 1.0 broadcast_multiply_fusion.1
  167.3 3.8 %fusion.29 = (bf16[512,4,1,768]{0,3,1,2:T(8,128)(2,1)}, bf16[512,4,1,768]{0,3,1,2:T(8,128)(2,1)}, bf16[512,4,1,768]{0,3,1,2:T(8,128)(2,1)}) fusion(bf16[512,4,384]{0,2,1:T(8,128)(2,1)S(1)} %copy-done.2, bf16[512,4,384]{0,2,1:T(8,128)(2,1)S(1)} %get-tuple-element.7, bf16[512,4,384]{0,2,1:T(8,128)(2,1)S(1)} %copy-done.4), kind=kLoop, calls=%fused_computation.34 | loop fusion | flops 17301504 | bytes 14155776 | tf_op jit(solution)/shard_map/stack | solution.py:72
  171.1 2.6 %stack.42 = f32[64,2,2,1,512]{4,3,2,1,0:T(1,128)} reshape(f32[64,4,512]{2,1,0:T(4,128)} %copy-done.5) | data formatting | bytes 1048576 | tf_op jit(solution)/shard_map/stack | solution.py:61
  173.7 1.5 stack.43
  175.2 3.9 %fusion.31 = f32[64,2,2,2,512]{4,3,2,1,0:T(2,128)} fusion(f32[64,2,2,2,512]{4,3,2,1,0:T(2,128)} %param.10, f32[64,2,2,1,512]{4,3,2,1,0:T(1,128)} %stack.43, f32[64,2,2,1,512]{4,3,2,1,0:T(1,128)} %stack.42, f32[64,2,2,512]{3,2,1,0:T(2,128)} %broadcast_multiply_fusion.1), kind=kLoop, calls=%fused_computation.38 | loop fusion | flops 786432 | bytes 3670016 | tf_op jit(solution)/shard_map/mul | solution.py:70
  179.1 18.7 %all-gather.2.cloned.1.call-done = bf16[512,4,2,512]{3,1,2,0:T(4,128)(2,1)} async-done(((bf16[64,4,2,512]{3,1,2,0:T(4,128)(2,1)}), bf16[512,4,2,512]{3,1,2,0:T(4,128)(2,1)}) %all-gather.2.cloned.1.call-update) | async-done | bytes 4194320 | tf_op jit(solution)/shard_map/all_gather | solution.py:76
  197.8 7.7 %fusion.24 = f32[512,4,768]{0,2,1:T(8,128)S(1)} fusion(bf16[512,4,2,512]{3,1,2,0:T(4,128)(2,1)} %all-gather.2.cloned.1.call-done, bf16[512,4,1,768]{0,3,1,2:T(8,128)(2,1)} %maximum_negate_fusion, bf16[512,4,1,768]{0,3,1,2:T(8,128)(2,1)} %get-tuple-element.8), kind=kOutput, calls=%fused_computation.33 | convolution fusion | flops 3224371200 | bytes 16777216 | tf_op jit(solution)/shard_map/rmwq,qmwk->rmk/dot_general | solution.py:77
  205.5 6.8 %fusion.19 = f32[512,4,768]{0,2,1:T(8,128)S(1)} fusion(bf16[512,4,2,512]{3,1,2,0:T(4,128)(2,1)} %all-gather.2.cloned.1.call-done, bf16[512,4,1,768]{0,3,1,2:T(8,128)(2,1)S(1)} %copy-done.6, bf16[512,4,1,768]{0,3,1,2:T(8,128)(2,1)} %get-tuple-element.12), kind=kOutput, calls=%fused_computation.32 | convolution fusion | flops 3224371200 | bytes 16777216 | tf_op jit(solution)/shard_map/rmwp,rmwk->pmk/dot_general | solution.py:80
  212.3 1.9 fusion.16
  214.2 0.4 fusion.36
  214.7 11.7 %psum.14 = f32[2,512]{1,0:T(2,128)S(1)} all-reduce(f32[2,512]{1,0:T(2,128)S(1)} %fusion.36), channel_id=1, replica_groups=mesh['dir'=8,'freq'=4] {'freq'}, use_global_device_ids=true, to_apply=%region_2.0 | all-reduce | flops 1024 | bytes 8192 | tf_op jit(solution)/shard_map/psum | solution.py:91
  226.3 1.2 multiply_reduce_fusion
  227.5 12.5 %psum.15 = f32[]{:T(128)} all-reduce(f32[]{:T(128)} %get-tuple-element.18), channel_id=1, replica_groups=mesh['dir'=8,'freq'=4] {'dir'}, use_global_device_ids=true, to_apply=%region_4.0 | all-reduce | flops 1 | bytes 8 | tf_op jit(solution)/shard_map/psum | solution.py:93
  240.7 0.6 multiply_subtract_fusion
  (38 shorter events, 0.3 us)
Async XLA Ops:
  7.2 219.2 %copy-start = (f32[512,512]{1,0:T(8,128)S(1)}, f32[512,512]{1,0:T(8,128)}, u32[]{:S(2)}) copy-start(f32[512,512]{1,0:T(8,128)} %param.13) | copy-start | bytes 3145732
  7.2 120.1 %all-reduce.3.cloned.1.call-start = ((), (), s32[]{:S(2)}) async-start(), calls=%async_computation.2 | async-start | bytes 8388608
  8.8 5.5 %copy-start.9 = (f32[2,512]{1,0:T(2,128)S(1)}, f32[2,512]{1,0:T(2,128)}, u32[]{:S(2)}) copy-start(f32[2,512]{1,0:T(2,128)} %param.12) | copy-start | bytes 12292
  8.8 5.5 %copy-start.10 = (s32[384]{0:T(512)S(1)}, s32[384]{0:T(512)}, u32[]{:S(2)}) copy-start(s32[384]{0:T(512)} %param.18) | copy-start | bytes 4612
  8.8 6.0 %copy-start.11 = (f32[2,2,512]{2,1,0:T(2,128)S(1)}, f32[2,2,512]{2,1,0:T(2,128)}, u32[]{:S(2)}) copy-start(f32[2,2,512]{2,1,0:T(2,128)} %param.14) | copy-start | bytes 24580
  8.8 6.0 %copy-start.12 = (f32[2,384]{1,0:T(2,128)S(1)}, f32[2,384]{1,0:T(2,128)}, u32[]{:S(2)}) copy-start(f32[2,384]{1,0:T(2,128)} %param.15) | copy-start | bytes 9220
  14.8 14.2 %slice-start = ((s8[6291456]{0:T(1024)(128)(4,1)}), s8[4194304]{0:T(1024)(128)(4,1)S(1)}, s32[]{:S(2)}) async-start(s8[6291456]{0:T(1024)(128)(4,1)} %bitcast.76), calls=%async_computation.3 | async-start | bytes 8388608
  14.9 14.2 %slice-start.1 = ((s8[6291456]{0:T(1024)(128)(4,1)}), s8[2097152]{0:T(1024)(128)(4,1)S(1)}, s32[]{:S(2)}) async-start(s8[6291456]{0:T(1024)(128)(4,1)} %bitcast.76), calls=%async_computation.4 | async-start | bytes 4194304
  32.3 2.4 copy-start.1
  43.6 0.9 copy-start.8
  43.6 2.4 copy-start.13
  132.7 13.1 %all-to-all-start = ((f32[8,1,16384]{2,1,0:T(1,128)}), f32[8,1,16384]{2,1,0:T(1,128)S(1)}, u32[]{:S(2)}, u32[]{:S(2)}) async-start(f32[8,1,16384]{2,1,0:T(1,128)} %reshape.106), calls=%async_computation | async-start | bytes 1048576 | tf_op jit(solution)/shard_map/all_to_all | solution.py:59
  136.2 61.6 %all-gather.2.cloned.1.call-start = ((), (), s32[]{:S(2)}) async-start(), calls=%async_computation.1 | async-start | bytes 4718592 | tf_op jit(solution)/shard_map/all_gather | solution.py:76
  145.9 0.8 copy-start.7
  158.4 0.8 copy-start.5
  161.9 5.4 %copy-start.2 = (bf16[512,4,384]{0,2,1:T(8,128)(2,1)S(1)}, bf16[512,4,384]{0,2,1:T(8,128)(2,1)}, u32[]{:S(2)}) copy-start(bf16[512,4,384]{0,2,1:T(8,128)(2,1)} %copy-done.1) | copy-start | bytes 4718596
  162.0 5.4 %copy-start.4 = (bf16[512,4,384]{0,2,1:T(8,128)(2,1)S(1)}, bf16[512,4,384]{0,2,1:T(8,128)(2,1)}, u32[]{:S(2)}) copy-start(bf16[512,4,384]{0,2,1:T(8,128)(2,1)} %get-tuple-element.4) | copy-start | bytes 4718596
  197.8 7.8 %copy-start.6 = (bf16[512,4,1,768]{0,3,1,2:T(8,128)(2,1)S(1)}, bf16[512,4,1,768]{0,3,1,2:T(8,128)(2,1)}, u32[]{:S(2)}) copy-start(bf16[512,4,1,768]{0,3,1,2:T(8,128)(2,1)} %get-tuple-element.9) | copy-start | bytes 9437188
  205.5 6.8 %copy-start.3 = (bf16[512,4,384]{0,2,1:T(8,128)(2,1)S(1)}, bf16[512,4,384]{0,2,1:T(8,128)(2,1)}, u32[]{:S(2)}) copy-start(bf16[512,4,384]{0,2,1:T(8,128)(2,1)} %copy-done.1) | copy-start | bytes 4718596
Sparse Core Ops, SparseCore 0:
  43.8 83.5 all-reduce.2
  162.1 35.6 all-gather.1
where the time goes:
time: 249 us; the launch traced here: 248 us
  waiting for transfers between devices  106 us (43%)
  matrix products  36.4 us (15%)
  local copies, waits for them, and re-layouts  34.8 us (14%)
  other arithmetic  27.3 us (11%)
  blocking collectives  24.1 us (10%)
  between operations  15.6 us (6%)
  starting transfers between devices  3.75 us (2%)
    unnamed x3, waiting for transfers between devices  80.1 us
    all_gather x1, waiting for transfers between devices, body(): rows_piece = lax.all_gather(resid_half, 'dir', axis=0, tiled=True)  18.7 us
    dot_general x1, matrix products, body(): geometry = jnp.einsum('mcp,ck->pmk', uv_each, source_lm, precision=highest)  14.2 us
    psum x1, blocking collectives, body(): total_sq = lax.psum(jnp.sum(smooth * smooth), 'dir')  12.5 us
    psum x1, blocking collectives, body(): total_grad = lax.psum(local_grad, 'freq')  11.7 us
    unnamed x36, local copies, waits for them, and re-layouts  8.85 us
    dot_general x1, matrix products, body(): jnp.einsum('rmwq,qmwk->rmk', rows_piece, forward_mat, preferred_element_t...  7.74 us
    all_to_all x1, waiting for transfers between devices, body(): lax.all_to_all(packed_rows, 'dir', split_axis=2, concat_axis=0, tiled=True)  7.36 us
  transfers between devices with their start and end apart: 3, of which 3 were waited for; matrix products, arithmetic and copies ran while one was open for 9% of the time, Pallas kernels for 0%

commit v1 on v0

--- a/solution.py
+++ b/solution.py
@@ -7,6 +7,15 @@
 step_size = 0.3
 epsilon = 1e-06
 highest = lax.Precision.HIGHEST
+
+
+def _do_tiles(local_block):
+    return jnp.concatenate(
+        lax.all_to_all(
+            jnp.stack(jnp.split(local_block, lax.psum(1, "dir"), axis=2), axis=0), "dir", 0, 0
+        ),
+        axis=0,
+    )
 
 
 def body(
@@ -56,7 +65,7 @@
     packed_rows = lax.psum_scatter(
         (real_part + imag_part) * scaling, "dir", scatter_dimension=0, tiled=True
     )
-    mirrored = lax.all_to_all(packed_rows, "dir", split_axis=2, concat_axis=0, tiled=True)
+    mirrored = _do_tiles(packed_rows)
     mirrored = jnp.transpose(mirrored, (2, 1, 0))
     model_rows = jnp.stack([(packed_rows + mirrored) * 0.5, (packed_rows - mirrored) * 0.5], axis=2)
     row_ids = lax.axis_index("dir") * local_rows + jnp.arange(local_rows, dtype=jnp.int32)

time: 249 us -> 258 us (1.036)
  local copies, waits for them, and re-layouts: 34.8 us -> 43.5 us
    unnamed x36 -> x40, local copies, waits for them, and re-layouts: 8.85 us -> 19 us
    all_to_all x3 -> x1, local copies, waits for them, and re-layouts: 5.69 us -> 0.51 us  [_do_tiles(): lax.all_to_all(jnp.stack(jnp.split(local_block, lax.psum(1, 'dir'), axis=...]
  transfers between devices with their start and end apart: 3 -> 3, of which waited for: 3 -> 3; matrix products, arithmetic and copies ran while one was open for 9% -> 8% of each run, Pallas kernels for 0% -> 0%
where the time goes in v1:
time: 258 us; the launch traced here: 257 us
  waiting for transfers between devices  106 us (41%)
  local copies, waits for them, and re-layouts  43.5 us (17%)
  matrix products  36.4 us (14%)
  other arithmetic  26.2 us (10%)
  blocking collectives  24.1 us (9%)
  between operations  15.7 us (6%)
  starting transfers between devices  4.41 us (2%)
    unnamed x3, waiting for transfers between devices  79 us
    unnamed x40, local copies, waits for them, and re-layouts  19 us
    all_gather x1, waiting for transfers between devices, body(): rows_piece = lax.all_gather(resid_half, 'dir', axis=0, tiled=True)  18.7 us
    dot_general x1, matrix products, body(): geometry = jnp.einsum('mcp,ck->pmk', uv_each, source_lm, precision=highest)  14.2 us
    psum x1, blocking collectives, body(): total_sq = lax.psum(jnp.sum(smooth * smooth), 'dir')  12.4 us
    psum x1, blocking collectives, body(): total_grad = lax.psum(local_grad, 'freq')  11.7 us
    all_to_all x1, waiting for transfers between devices, _do_tiles(): lax.all_to_all(jnp.stack(jnp.split(local_block, lax.psum(1, 'dir'), axis=...  8.67 us
    dot_general x1, matrix products, body(): jnp.einsum('rmwq,qmwk->rmk', rows_piece, forward_mat, preferred_element_t...  7.73 us
  transfers between devices with their start and end apart: 3, of which 3 were waited for; matrix products, arithmetic and copies ran while one was open for 8% of the time, Pallas kernels for 0%

profile of v1, /device:TPU:0, one launch (start us, length us, event | category | flops | bytes accessed | tf_op | source)
XLA Modules:
  0.0 256.7 jit_solution(3317104095394393499)
XLA Ops:
  7.2 0.8 broadcast_in_dim.2
  8.1 0.7 sqrt.3
  8.8 5.5 %copy.27 = f32[2,2,2,512,384]{3,4,1,0,2:T(8,128)} copy(bf16[2,2,2,512,384]{4,3,2,1,0:T(8,128)(2,1)} %param.17) | data formatting | bytes 9437184 | tf_op jit(solution)/shard_map/convert_element_type | solution.py:53
  14.3 0.5 convolution_bitcast_fusion
  14.9 14.2 %fusion.54 = (f32[512,4,384]{0,2,1:T(8,128)S(1)}, f32[512,4,384]{0,2,1:T(8,128)S(1)}) fusion(f32[4,2,512]{2,1,0:T(2,128)S(1)} %bitcast.107, f32[2,384]{1,0:T(2,128)S(1)} %copy-done.11, f32[4]{0:T(128)S(1)} %get-tuple-element.16, f32[4]{0:T(128)S(1)} %div.26, f32[512,384]{0,1:T(8,128)S(1)} %convolution_bitcast_fusion), kind=kOutput, calls=%fused_computation.82 | convolution fusion | flops 21233664 | bytes 7097376 | tf_op jit(solution)/shard_map/mcp,ck->pmk/dot_general | solution.py:48
  29.1 3.2 %fusion.53 = (bf16[512,4,384]{0,2,1:T(8,128)(2,1)}, bf16[512,4,384]{0,2,1:T(8,128)(2,1)S(1)}, bf16[512,4,1,384]{0,3,1,2:T(8,128)(2,1)}, bf16[512,4,384]{0,2,1:T(8,128)(2,1)S(1)}) fusion(f32[512,4,384]{0,2,1:T(8,128)S(1)} %get-tuple-element.12, f32[4,2,512,384]{2,3,0,1:T(8,128)S(1)} %bitcast.101, f32[512,4,384]{0,2,1:T(8,128)S(1)} %get-tuple-element.13, ...), kind=kLoop, calls=%fused_computation.81 | loop fusion | flops 9437184 | bytes 18875904 | tf_op jit(solution)/shard_map/neg | solution.py:82
  32.5 2.1 fusion.30
  34.6 3.4 %multiply_bitcast_fusion = f32[512,4,512]{0,2,1:T(8,128)} fusion(f32[4,512,512]{2,1,0:T(8,128)S(1)} %fusion.30, bf16[512,4,384]{0,2,1:T(8,128)(2,1)S(1)} %get-tuple-element.5, bf16[512,4,384]{0,2,1:T(8,128)(2,1)S(1)} %neg.16, bf16[512,4,384]{0,2,1:T(8,128)(2,1)S(1)} %get-tuple-element.7), kind=kOutput, calls=%fused_computation.8 | convolution fusion | flops 1625292800 | bytes 13107200 | tf_op jit(solution)/shard_map/pmk,qmk->pmq/dot_general | solution.py:64
  38.1 5.5 %copy.32 = f32[512,4,512]{2,1,0:T(4,128)} copy(f32[512,4,512]{0,2,1:T(8,128)} %multiply_bitcast_fusion) | data formatting | bytes 8388608 | tf_op jit(solution)/shard_map/mul | solution.py:66
  43.6 0.9 copy-done.7
  44.6 0.9 tile.6
  45.5 1.5 convert_element_type.49
  47.0 0.6 dynamic-slice
  48.3 79.0 %all-reduce.3.cloned.1.call-done = f32[512,4,512]{2,1,0:T(4,128)} async-done(((f32[512,4,512]{2,1,0:T(4,128)}), f32[512,4,512]{2,1,0:T(4,128)}) %all-reduce.3.cloned.1.call-update) | async-done | bytes 4194320
  127.3 1.6 fusion.44
  128.8 1.7 fusion.43
  130.6 1.7 fusion.42
  132.3 1.7 fusion.41
  134.1 1.7 fusion.40
  135.8 1.7 fusion.39
  137.5 1.7 fusion.38
  139.2 1.7 fusion.37
  140.9 3.0 %reshape.110 = f32[8,1,16384]{2,1,0:T(1,128)} reshape(f32[8,64,4,64]{3,2,1,0:T(4,128)} %fusion.37) | data formatting | bytes 1048576
  144.0 4.3 %all-to-all-start = ((f32[8,1,16384]{2,1,0:T(1,128)}), f32[8,1,16384]{2,1,0:T(1,128)}, u32[]{:S(2)}, u32[]{:S(2)}) async-start(f32[8,1,16384]{2,1,0:T(1,128)} %reshape.110), calls=%async_computation | async-start | bytes 1048576 | tf_op jit(solution)/shard_map/all_to_all | solution.py:14
  148.4 0.9 broadcast_multiply_fusion
  149.4 8.7 %all-to-all-done = f32[8,1,16384]{2,1,0:T(1,128)} async-done(((f32[8,1,16384]{2,1,0:T(1,128)}), f32[8,1,16384]{2,1,0:T(1,128)}, u32[]{:S(2)}, u32[]{:S(2)}) %all-to-all-start) | async-done | bytes 524320 | tf_op jit(solution)/shard_map/all_to_all | solution.py:14
  158.0 0.5 broadcast.60
  158.5 2.9 %reduce = f32[8,16384]{1,0:T(8,128)S(1)} reduce(f32[8,1,16384]{2,1,0:T(1,128)} %all-to-all-done, f32[]{:T(128)} %broadcast.60), dimensions={1}, to_apply=%all_to_all.3.reduce_sub_computation | reduce | bytes 1048580 | tf_op jit(solution)/shard_map/all_to_all | solution.py:14
  161.5 1.7 reshape.111
  163.1 2.4 copy.50
  165.5 1.4 fusion.34
  166.9 0.8 copy-done.5
  167.7 1.8 fusion.33
  169.5 1.0 copy.37
  170.5 4.4 %maximum_negate_fusion = bf16[512,4,1,768]{0,3,1,2:T(8,128)(2,1)} fusion(bf16[512,4,1,384]{0,3,1,2:T(8,128)(2,1)} %get-tuple-element.6, bf16[512,4,1,384]{0,3,1,2:T(8,128)(2,1)} %bitcast.102), kind=kLoop, calls=%fused_computation.29 | loop fusion | flops 7864320 | bytes 6291456 | tf_op jit(solution)/shard_map/neg | solution.py:81
  174.9 1.0 broadcast_multiply_fusion.1
  175.9 3.8 %fusion.29 = (bf16[512,4,1,768]{0,3,1,2:T(8,128)(2,1)}, bf16[512,4,1,768]{0,3,1,2:T(8,128)(2,1)}, bf16[512,4,1,768]{0,3,1,2:T(8,128)(2,1)}) fusion(bf16[512,4,384]{0,2,1:T(8,128)(2,1)S(1)} %copy-done.2, bf16[512,4,384]{0,2,1:T(8,128)(2,1)S(1)} %get-tuple-element.7, bf16[512,4,384]{0,2,1:T(8,128)(2,1)S(1)} %copy-done.4), kind=kLoop, calls=%fused_computation.34 | loop fusion | flops 17301504 | bytes 14155776 | tf_op jit(solution)/shard_map/stack | solution.py:81
  179.6 2.6 %stack.78 = f32[64,2,2,1,512]{4,3,2,1,0:T(1,128)} reshape(f32[64,4,512]{2,1,0:T(4,128)} %copy-done.5) | data formatting | bytes 1048576 | tf_op jit(solution)/shard_map/stack | solution.py:70
  182.2 1.5 stack.79
  183.7 3.9 %fusion.31 = f32[64,2,2,2,512]{4,3,2,1,0:T(2,128)} fusion(f32[64,2,2,2,512]{4,3,2,1,0:T(2,128)} %param.10, f32[64,2,2,1,512]{4,3,2,1,0:T(1,128)} %stack.79, f32[64,2,2,1,512]{4,3,2,1,0:T(1,128)} %stack.78, f32[64,2,2,512]{3,2,1,0:T(2,128)} %broadcast_multiply_fusion.1), kind=kLoop, calls=%fused_computation.38 | loop fusion | flops 786432 | bytes 3670016 | tf_op jit(solution)/shard_map/mul | solution.py:79
  187.7 18.7 %all-gather.2.cloned.1.call-done = bf16[512,4,2,512]{3,1,2,0:T(4,128)(2,1)} async-done(((bf16[64,4,2,512]{3,1,2,0:T(4,128)(2,1)}), bf16[512,4,2,512]{3,1,2,0:T(4,128)(2,1)}) %all-gather.2.cloned.1.call-update) | async-done | bytes 4194320 | tf_op jit(solution)/shard_map/all_gather | solution.py:85
  206.3 7.7 %fusion.24 = f32[512,4,768]{0,2,1:T(8,128)S(1)} fusion(bf16[512,4,2,512]{3,1,2,0:T(4,128)(2,1)} %all-gather.2.cloned.1.call-done, bf16[512,4,1,768]{0,3,1,2:T(8,128)(2,1)} %maximum_negate_fusion, bf16[512,4,1,768]{0,3,1,2:T(8,128)(2,1)} %get-tuple-element.10), kind=kOutput, calls=%fused_computation.33 | convolution fusion | flops 3224371200 | bytes 16777216 | tf_op jit(solution)/shard_map/rmwq,qmwk->rmk/dot_general | solution.py:86
  214.1 6.8 %fusion.19 = f32[512,4,768]{0,2,1:T(8,128)S(1)} fusion(bf16[512,4,2,512]{3,1,2,0:T(4,128)(2,1)} %all-gather.2.cloned.1.call-done, bf16[512,4,1,768]{0,3,1,2:T(8,128)(2,1)S(1)} %copy-done.6, bf16[512,4,1,768]{0,3,1,2:T(8,128)(2,1)} %get-tuple-element.14), kind=kOutput, calls=%fused_computation.32 | convolution fusion | flops 3224371200 | bytes 16777216 | tf_op jit(solution)/shard_map/rmwp,rmwk->pmk/dot_general | solution.py:89
  220.9 1.9 fusion.16
  223.2 11.7 %psum.14 = f32[2,512]{1,0:T(2,128)S(1)} all-reduce(f32[2,512]{1,0:T(2,128)S(1)} %fusion.36), channel_id=1, replica_groups=mesh['dir'=8,'freq'=4] {'freq'}, use_global_device_ids=true, to_apply=%region_2.0 | all-reduce | flops 1024 | bytes 8192 | tf_op jit(solution)/shard_map/psum | solution.py:100
  234.9 1.2 multiply_reduce_fusion
  236.1 12.4 %psum.15 = f32[]{:T(128)} all-reduce(f32[]{:T(128)} %get-tuple-element.18), channel_id=1, replica_groups=mesh['dir'=8,'freq'=4] {'dir'}, use_global_device_ids=true, to_apply=%region_4.0 | all-reduce | flops 1 | bytes 8 | tf_op jit(solution)/shard_map/psum | solution.py:102
  249.2 0.6 multiply_subtract_fusion
  (41 shorter events, 1.2 us)
Async XLA Ops:
  7.2 227.7 %copy-start = (f32[512,512]{1,0:T(8,128)S(1)}, f32[512,512]{1,0:T(8,128)}, u32[]{:S(2)}) copy-start(f32[512,512]{1,0:T(8,128)} %param.13) | copy-start | bytes 3145732
  7.2 120.1 %all-reduce.3.cloned.1.call-start = ((), (), s32[]{:S(2)}) async-start(), calls=%async_computation.2 | async-start | bytes 8388608
  8.8 5.5 %copy-start.8 = (f32[2,512]{1,0:T(2,128)S(1)}, f32[2,512]{1,0:T(2,128)}, u32[]{:S(2)}) copy-start(f32[2,512]{1,0:T(2,128)} %param.12) | copy-start | bytes 12292
  8.8 5.5 %copy-start.9 = (s32[384]{0:T(512)S(1)}, s32[384]{0:T(512)}, u32[]{:S(2)}) copy-start(s32[384]{0:T(512)} %param.18) | copy-start | bytes 4612
  8.8 6.0 %copy-start.10 = (f32[2,2,512]{2,1,0:T(2,128)S(1)}, f32[2,2,512]{2,1,0:T(2,128)}, u32[]{:S(2)}) copy-start(f32[2,2,512]{2,1,0:T(2,128)} %param.14) | copy-start | bytes 24580
  8.8 6.0 %copy-start.11 = (f32[2,384]{1,0:T(2,128)S(1)}, f32[2,384]{1,0:T(2,128)}, u32[]{:S(2)}) copy-start(f32[2,384]{1,0:T(2,128)} %param.15) | copy-start | bytes 9220
  14.8 14.2 %slice-start = ((s8[6291456]{0:T(1024)(128)(4,1)}), s8[4194304]{0:T(1024)(128)(4,1)S(1)}, s32[]{:S(2)}) async-start(s8[6291456]{0:T(1024)(128)(4,1)} %bitcast.99), calls=%async_computation.3 | async-start | bytes 8388608
  14.9 14.2 %slice-start.1 = ((s8[6291456]{0:T(1024)(128)(4,1)}), s8[2097152]{0:T(1024)(128)(4,1)S(1)}, s32[]{:S(2)}) async-start(s8[6291456]{0:T(1024)(128)(4,1)} %bitcast.99), calls=%async_computation.4 | async-start | bytes 4194304
  32.2 2.4 copy-start.1
  43.5 0.9 copy-start.7
  43.6 3.5 %copy-start.12 = (u32[32]{0:T(128)S(1)}, u32[32]{0:T(128)}, u32[]{:S(2)}) copy-start(u32[32]{0:T(128)} %constant.30) | copy-start | bytes 388
  144.0 14.1 %all-to-all-start = ((f32[8,1,16384]{2,1,0:T(1,128)}), f32[8,1,16384]{2,1,0:T(1,128)}, u32[]{:S(2)}, u32[]{:S(2)}) async-start(f32[8,1,16384]{2,1,0:T(1,128)} %reshape.110), calls=%async_computation | async-start | bytes 1048576 | tf_op jit(solution)/shard_map/all_to_all | solution.py:14
  148.3 58.0 %all-gather.2.cloned.1.call-start = ((), (), s32[]{:S(2)}) async-start(), calls=%async_computation.1 | async-start | bytes 4718592 | tf_op jit(solution)/shard_map/all_gather | solution.py:85
  166.9 0.8 copy-start.5
  170.5 5.4 %copy-start.2 = (bf16[512,4,384]{0,2,1:T(8,128)(2,1)S(1)}, bf16[512,4,384]{0,2,1:T(8,128)(2,1)}, u32[]{:S(2)}) copy-start(bf16[512,4,384]{0,2,1:T(8,128)(2,1)} %copy-done.1) | copy-start | bytes 4718596
  170.5 5.4 %copy-start.4 = (bf16[512,4,384]{0,2,1:T(8,128)(2,1)S(1)}, bf16[512,4,384]{0,2,1:T(8,128)(2,1)}, u32[]{:S(2)}) copy-start(bf16[512,4,384]{0,2,1:T(8,128)(2,1)} %get-tuple-element.4) | copy-start | bytes 4718596
  206.3 7.7 %copy-start.6 = (bf16[512,4,1,768]{0,3,1,2:T(8,128)(2,1)S(1)}, bf16[512,4,1,768]{0,3,1,2:T(8,128)(2,1)}, u32[]{:S(2)}) copy-start(bf16[512,4,1,768]{0,3,1,2:T(8,128)(2,1)} %get-tuple-element.11) | copy-start | bytes 9437188
  214.1 6.8 %copy-start.3 = (bf16[512,4,384]{0,2,1:T(8,128)(2,1)S(1)}, bf16[512,4,384]{0,2,1:T(8,128)(2,1)}, u32[]{:S(2)}) copy-start(bf16[512,4,384]{0,2,1:T(8,128)(2,1)} %copy-done.1) | copy-start | bytes 4718596
Sparse Core Ops, SparseCore 0:
  43.7 83.5 all-reduce.2
  170.6 35.6 all-gather.1
